TPU v7x, 512 devices: a whole 4x8x8 slice. The times are simulated.
512 devices in a mesh: st: 8 (over x, core), fsdp: 64 (over z, y).
Axes of the slice: x: 4, y: 8, z: 8, core: 2. Of those that a mesh axis runs over, the one named last changes fastest.
Arguments:
- normed: bfloat16 [64, 512, 3072], P('fsdp')
- qkv_weight: bfloat16 [3072, 32, 384], P('fsdp', 'st'), may hold values from -0.109375 to 0.109375
- out_weight: bfloat16 [3072, 4096], P('fsdp', 'st'), may hold values from -0.09375 to 0.09375
- segment_ids: int32 [64], replicated, may hold values from 0 to 15, never falling along the last dimension, each value on 1 to 8 neighbouring positions
Outputs:
- attended: bfloat16 [64, 512, 3072], P('fsdp', 'st')
Inputs may be any that keep to these rules, and one draw needn't show every extreme that they name: `segment_ids`: segment ids never fall from one frame to the next; each clip covers 1 to 8 consecutive frames, and one covers exactly 8.
All inputs are finite; a program needn't handle non-finite values.
Results may differ from a plain program's by a relative error of at most 0.017.
Values may be sent and summed in bfloat16 or wider, within the bound.
A program may use at most 64 MiB of HBM per device.

v0:
```python
import math
import jax
import jax.numpy as jnp
from jax import lax
from jax.sharding import PartitionSpec as P

HEAD = 128
HS_DEV = 2


def softmax_rows(scores):
    top = jnp.max(scores, axis=-1, keepdims=True)
    expo = jnp.exp(scores - top)
    return expo / jnp.sum(expo, axis=-1, keepdims=True)


def shards(normed, qkv_weight, out_weight, segment_ids):
    patches = normed.shape[1]
    width = normed.shape[2]
    group = qkv_weight.shape[1]
    scale = 1.0 / math.sqrt(HEAD)
    frame_rows = normed.reshape(patches, width)
    projected = jnp.einsum(
        "pd,dhc->phc",
        frame_rows,
        lax.all_gather(qkv_weight, "fsdp", axis=0, tiled=True),
        preferred_element_type=jnp.float32,
    )
    out_full = lax.all_gather(out_weight, "fsdp", axis=0, tiled=True)
    packed = projected.astype(jnp.bfloat16)
    spatial = packed[:, :HS_DEV]
    scores = (
        jnp.einsum(
            "qhc,khc->hqk",
            spatial[..., :HEAD],
            spatial[..., HEAD : 2 * HEAD],
            preferred_element_type=jnp.float32,
        )
        * scale
    )
    weights = softmax_rows(scores).astype(jnp.bfloat16)
    spatial_out = jnp.einsum(
        "hqk,khc->qhc", weights, spatial[..., 2 * HEAD :], preferred_element_type=jnp.float32
    ).astype(jnp.bfloat16)
    temporal_in = packed[:, HS_DEV:].reshape(1, patches, group - HS_DEV, 3 * HEAD)
    block = lax.all_to_all(temporal_in, "fsdp", split_axis=1, concat_axis=0, tiled=True)
    query = block[..., :HEAD]
    keys = block[..., HEAD : 2 * HEAD]
    values = block[..., 2 * HEAD :]
    all_scores = (
        jnp.einsum("tphc,uphc->phtu", query, keys, preferred_element_type=jnp.float32) * scale
    )
    same = segment_ids[:, None] == segment_ids[None, :]
    all_scores = jnp.where(same, all_scores, jnp.float32(-1e30))
    all_weights = softmax_rows(all_scores).astype(jnp.bfloat16)
    result = jnp.einsum("phtu,uphc->tphc", all_weights, values, preferred_element_type=jnp.float32)
    temporal_out = lax.all_to_all(
        result.astype(jnp.bfloat16), "fsdp", split_axis=0, concat_axis=1, tiled=True
    )
    heads_out = jnp.concatenate(
        [spatial_out, temporal_out.reshape(patches, group - HS_DEV, HEAD)], axis=1
    )
    heads_out = heads_out.reshape(patches, group * HEAD)
    summed = lax.psum_scatter(
        lax.dot_general(
            heads_out, out_full, (((1,), (1,)), ((), ())), preferred_element_type=jnp.float32
        ).astype(jnp.bfloat16),
        "st",
        scatter_dimension=0,
        tiled=True,
    ).astype(jnp.float32)
    return summed.astype(jnp.bfloat16).reshape(1, summed.shape[0], width)


def solution(mesh):
    return jax.shard_map(
        shards,
        mesh=mesh,
        in_specs=(P("fsdp", None, None), P("fsdp", "st", None), P("fsdp", "st"), P()),
        out_specs=P("fsdp", "st", None),
        check_vma=False,
    )
```

profile of v0, /device:TPU:8, one launch (start us, length us, event | category | flops | bytes accessed | tf_op | source)
XLA Modules:
  0.0 264.6 jit_solution(5956684058588850839)
XLA Ops:
  6.5 0.0 copy-start
  6.5 0.0 all-gather.3.cloned.1.call-start
  6.5 1.7 copy.30
  8.3 0.0 all-gather.3.cloned.1.call-update
  8.3 0.0 all-gather.5.cloned.1.call-start
  8.4 0.7 all-gather.5.cloned.1.call-update
  9.1 110.5 %all-gather.3.cloned.1.call-done = bf16[3072,4,384]{2,0,1:T(8,128)(2,1)} async-done(((bf16[48,4,384]{2,0,1:T(8,128)(2,1)}), bf16[3072,4,384]{2,0,1:T(8,128)(2,1)}) %all-gather.3.cloned.1.call-update) | async-done | bytes 9437200 | tf_op jit(solution)/shard_map/all_gather | solution.py:26
  119.6 0.0 copy-done
  119.6 7.8 %fusion.5 = bf16[512,4,384]{2,0,1:T(8,128)(2,1)S(1)} fusion(bf16[3072,4,384]{2,0,1:T(8,128)(2,1)} %all-gather.3.cloned.1.call-done, bf16[1,512,3072]{2,1,0:T(8,128)(2,1)S(1)} %copy-done), kind=kOutput, calls=%fused_computation.9 | convolution fusion | flops 4832624640 | bytes 14155776 | tf_op jit(solution)/shard_map/pd,dhc->phc/dot_general | solution.py:23
  127.3 0.0 copy-start.1
  127.3 1.1 copy-done.1
  128.5 0.0 copy-start.2
  128.5 0.1 slice_bitcast_fusion
  128.6 1.7 copy.33
  130.3 10.3 %all-to-all-start = ((bf16[1,512,2,384]{3,2,0,1:T(2,128)(2,1)}), bf16[1,512,2,384]{3,2,0,1:T(2,128)(2,1)}, u32[]{:S(2)}, u32[]{:S(2)}) async-start(bf16[1,512,2,384]{3,2,0,1:T(2,128)(2,1)} %copy.33), calls=%async_computation | async-start | bytes 1572864 | tf_op jit(solution)/shard_map/all_to_all | solution.py:46
  140.6 0.0 copy-done.2
  140.6 0.1 broadcast_compare_fusion
  140.7 24.8 %all-to-all-done = bf16[1,512,2,384]{3,2,0,1:T(2,128)(2,1)} async-done(((bf16[1,512,2,384]{3,2,0,1:T(2,128)(2,1)}), bf16[1,512,2,384]{3,2,0,1:T(2,128)(2,1)}, u32[]{:S(2)}, u32[]{:S(2)}) %all-to-all-start) | async-done | bytes 786464 | tf_op jit(solution)/shard_map/all_to_all | solution.py:46
  165.5 1.2 copy.57
  166.8 0.8 fusion.51
  167.6 0.3 fusion.10
  167.9 0.0 copy-start.3
  167.9 0.1 fusion.52
  168.0 0.7 copy-done.3
  168.7 1.6 fusion.11
  170.3 1.0 copy.39
  171.3 6.5 %all-to-all-start.1 = ((bf16[64,8,2,128]{3,2,1,0:T(2,128)(2,1)}), bf16[64,8,2,128]{3,2,1,0:T(2,128)(2,1)S(1)}, u32[]{:S(2)}, u32[]{:S(2)}) async-start(bf16[64,8,2,128]{3,2,1,0:T(2,128)(2,1)} %copy.39), calls=%async_computation.1 | async-start | bytes 524288 | tf_op jit(solution)/shard_map/all_to_all | solution.py:57
  177.8 0.0 reduce-scatter.2.cloned.1.call-start
  177.8 1.8 fusion.53
  179.7 3.0 %fusion.12 = bf16[512,2,128]{0,2,1:T(8,128)(2,1)} fusion(f32[2,512]{1,0:T(2,128)S(1)} %fusion.53, bf16[512,4,384]{2,0,1:T(8,128)(2,1)} %copy-done.1), kind=kOutput, calls=%fused_computation.17 | convolution fusion | flops 270665216 | bytes 1052672 | tf_op jit(solution)/shard_map/hqk,khc->qhc/dot_general | solution.py:42
  182.6 8.8 %all-to-all-done.1 = bf16[64,8,2,128]{3,2,1,0:T(2,128)(2,1)S(1)} async-done(((bf16[64,8,2,128]{3,2,1,0:T(2,128)(2,1)}), bf16[64,8,2,128]{3,2,1,0:T(2,128)(2,1)S(1)}, u32[]{:S(2)}, u32[]{:S(2)}) %all-to-all-start.1) | async-done | bytes 262176 | tf_op jit(solution)/shard_map/all_to_all | solution.py:57
  191.4 0.9 copy.41
  192.3 1.9 pad_maximum_fusion
  194.2 19.5 %all-gather.5.cloned.1.call-done = bf16[3072,512]{1,0:T(8,128)(2,1)} async-done(((bf16[48,512]{1,0:T(8,128)(2,1)}), bf16[3072,512]{1,0:T(8,128)(2,1)}) %all-gather.5.cloned.1.call-update) | async-done | bytes 3145744 | tf_op jit(solution)/shard_map/all_gather | solution.py:29
  213.7 5.6 %convolution_convert_fusion = bf16[512,3072]{1,0:T(8,128)(2,1)} fusion(bf16[512,512]{0,1:T(8,128)(2,1)} %bitcast.25, bf16[3072,512]{1,0:T(8,128)(2,1)} %all-gather.5.cloned.1.call-done), kind=kOutput, calls=%fused_computation.2 | convolution fusion | flops 1612185600 | bytes 6815744 | tf_op jit(solution)/shard_map/dot_general | solution.py:65
  219.3 0.0 reduce-scatter.2.cloned.1.call-update
  219.3 38.8 %reduce-scatter.2.cloned.1.call-done = bf16[64,3072]{1,0:T(8,128)(2,1)} async-done(((bf16[512,3072]{1,0:T(8,128)(2,1)}), bf16[64,3072]{1,0:T(8,128)(2,1)}) %reduce-scatter.2.cloned.1.call-update) | async-done | bytes 393232 | tf_op jit(solution)/shard_map/reduce_scatter | solution.py:64
Async XLA Ops:
  6.5 113.0 %copy-start = (bf16[1,512,3072]{2,1,0:T(8,128)(2,1)S(1)}, bf16[1,512,3072]{2,1,0:T(8,128)(2,1)}, u32[]{:S(2)}) copy-start(bf16[1,512,3072]{2,1,0:T(8,128)(2,1)} %param.4) | copy-start | bytes 9437188
  6.5 113.0 %all-gather.3.cloned.1.call-start = ((), (), s32[]{:S(2)}) async-start(), calls=%async_computation.3 | async-start | bytes 9584640 | tf_op jit(solution)/shard_map/all_gather | solution.py:26
  8.3 205.4 %all-gather.5.cloned.1.call-start = ((), (), s32[]{:S(2)}) async-start(), calls=%async_computation.4 | async-start | bytes 3194880 | tf_op jit(solution)/shard_map/all_gather | solution.py:29
  127.3 1.2 copy-start.1
  128.5 12.1 %copy-start.2 = (s32[64]{0:T(128)S(1)}, s32[64]{0:T(128)}, u32[]{:S(2)}) copy-start(s32[64]{0:T(128)} %param.7) | copy-start | bytes 772
  130.3 35.3 %all-to-all-start = ((bf16[1,512,2,384]{3,2,0,1:T(2,128)(2,1)}), bf16[1,512,2,384]{3,2,0,1:T(2,128)(2,1)}, u32[]{:S(2)}, u32[]{:S(2)}) async-start(bf16[1,512,2,384]{3,2,0,1:T(2,128)(2,1)} %copy.33), calls=%async_computation | async-start | bytes 1572864 | tf_op jit(solution)/shard_map/all_to_all | solution.py:46
  167.9 0.8 copy-start.3
  171.3 20.2 %all-to-all-start.1 = ((bf16[64,8,2,128]{3,2,1,0:T(2,128)(2,1)}), bf16[64,8,2,128]{3,2,1,0:T(2,128)(2,1)S(1)}, u32[]{:S(2)}, u32[]{:S(2)}) async-start(bf16[64,8,2,128]{3,2,1,0:T(2,128)(2,1)} %copy.39), calls=%async_computation.1 | async-start | bytes 524288 | tf_op jit(solution)/shard_map/all_to_all | solution.py:57
  177.8 80.3 %reduce-scatter.2.cloned.1.call-start = ((), (), s32[]{:S(2)}) async-start(), calls=%async_computation.5 | async-start | bytes 3538944 | tf_op jit(solution)/shard_map/reduce_scatter | solution.py:64
Sparse Core Ops, SparseCore 0:
  10.4 109.0 all-gather.2
  122.6 91.1 all-gather.4
  219.4 38.6 reduce-scatter.1
where the time goes:
time: 265 us
  waiting for transfers between devices  203 us (77%)
  matrix products  20 us (8%)
  starting transfers between devices  16.9 us (6%)
  between operations  13.2 us (5%)
  local copies, waits for them, and re-layouts  9.24 us (3%)
    all_gather x1, waiting for transfers between devices, shards(): lax.all_gather(qkv_weight, 'fsdp', axis=0, tiled=True)  111 us
    reduce_scatter x1, waiting for transfers between devices, shards(): lax.psum_scatter(lax.dot_general(heads_out, out_full, (((1,), (1,)), ((),...  38.8 us
    all_to_all x1, waiting for transfers between devices, shards(): lax.all_to_all(temporal_in, 'fsdp', split_axis=1, concat_axis=0, tiled=True)  24.8 us
    all_gather x1, waiting for transfers between devices, shards(): out_full = lax.all_gather(out_weight, 'fsdp', axis=0, tiled=True)  19.5 us
    all_to_all x1, starting transfers between devices, shards(): lax.all_to_all(temporal_in, 'fsdp', split_axis=1, concat_axis=0, tiled=True)  10.3 us
    all_to_all x1, waiting for transfers between devices, shards(): lax.all_to_all(result.astype(jnp.bfloat16), 'fsdp', split_axis=0, concat_...  8.82 us
    dot_general x1, matrix products, shards(): jnp.einsum('pd,dhc->phc', frame_rows, lax.all_gather(qkv_weight, 'fsdp',...  7.75 us
    all_to_all x1, starting transfers between devices, shards(): lax.all_to_all(result.astype(jnp.bfloat16), 'fsdp', split_axis=0, concat_...  6.5 us
  transfers between devices with their start and end apart: 5, of which 5 were waited for; matrix products, arithmetic and copies ran while one was open for 8% of the time, Pallas kernels for 0%

commit v1 on v0

--- a/solution.py
+++ b/solution.py
@@ -54,8 +54,14 @@
     all_scores = jnp.where(same, all_scores, jnp.float32(-1e30))
     all_weights = softmax_rows(all_scores).astype(jnp.bfloat16)
     result = jnp.einsum("phtu,uphc->tphc", all_weights, values, preferred_element_type=jnp.float32)
-    temporal_out = lax.all_to_all(
-        result.astype(jnp.bfloat16), "fsdp", split_axis=0, concat_axis=1, tiled=True
+    temporal_out = jnp.concatenate(
+        lax.all_to_all(
+            jnp.stack(jnp.split(result.astype(jnp.bfloat16), lax.axis_size("fsdp"), axis=0)),
+            "fsdp",
+            0,
+            0,
+        ),
+        axis=1,
     )
     heads_out = jnp.concatenate(
         [spatial_out, temporal_out.reshape(patches, group - HS_DEV, HEAD)], axis=1

time: 265 us -> 286 us (1.079)
  local copies, waits for them, and re-layouts: 9.24 us -> 47 us
  waiting for transfers between devices: 203 us -> 186 us
    unnamed x9 -> x72, local copies, waits for them, and re-layouts: 3.55 us -> 41.1 us
    all_gather x1, waiting for transfers between devices: 19.5 us -> 0.01 us  [shards(): out_full = lax.all_gather(out_weight, 'fsdp', axis=0, tiled=True)]
  transfers between devices with their start and end apart: 5 -> 5, of which waited for: 5 -> 4; matrix products, arithmetic and copies ran while one was open for 8% -> 18% of each run, Pallas kernels for 0% -> 0%
where the time goes in v1:
time: 286 us; the launch traced here: 285 us
  waiting for transfers between devices  186 us (65%)
  local copies, waits for them, and re-layouts  47 us (16%)
  matrix products  20 us (7%)
  starting transfers between devices  17 us (6%)
  between operations  13.3 us (5%)
    all_gather x1, waiting for transfers between devices, shards(): lax.all_gather(qkv_weight, 'fsdp', axis=0, tiled=True)  111 us
    unnamed x72, local copies, waits for them, and re-layouts  41.1 us
    reduce_scatter x1, waiting for transfers between devices, shards(): lax.psum_scatter(lax.dot_general(heads_out, out_full, (((1,), (1,)), ((),...  39.3 us
    all_to_all x1, waiting for transfers between devices, shards(): lax.all_to_all(temporal_in, 'fsdp', split_axis=1, concat_axis=0, tiled=True)  23.1 us
    all_to_all x1, waiting for transfers between devices, shards(): lax.all_to_all(jnp.stack(jnp.split(result.astype(jnp.bfloat16), lax.axis_...  11.6 us
    all_to_all x1, starting transfers between devices, shards(): lax.all_to_all(temporal_in, 'fsdp', split_axis=1, concat_axis=0, tiled=True)  10.3 us
    dot_general x1, matrix products, shards(): jnp.einsum('pd,dhc->phc', frame_rows, lax.all_gather(qkv_weight, 'fsdp',...  7.76 us
    all_to_all x1, starting transfers between devices, shards(): lax.all_to_all(jnp.stack(jnp.split(result.astype(jnp.bfloat16), lax.axis_...  6.56 us
  transfers between devices with their start and end apart: 5, of which 4 were waited for; matrix products, arithmetic and copies ran while one was open for 18% of the time, Pallas kernels for 0%

profile of v1, /device:TPU:8, one launch (start us, length us, event | category | flops | bytes accessed | tf_op | source)
XLA Modules:
  0.0 285.3 jit_solution(1657246578424658645)
XLA Ops:
  6.5 1.7 copy.2772
  8.3 111.3 %all-gather.3.cloned.1.call-done = bf16[3072,4,384]{2,0,1:T(8,128)(2,1)} async-done(((bf16[48,4,384]{2,0,1:T(8,128)(2,1)}), bf16[3072,4,384]{2,0,1:T(8,128)(2,1)}) %all-gather.3.cloned.1.call-update) | async-done | bytes 9437200 | tf_op jit(solution)/shard_map/all_gather | solution.py:26
  119.6 7.8 %fusion.5 = bf16[512,4,384]{2,0,1:T(8,128)(2,1)S(1)} fusion(bf16[3072,4,384]{2,0,1:T(8,128)(2,1)} %all-gather.3.cloned.1.call-done, bf16[1,512,3072]{2,1,0:T(8,128)(2,1)S(1)} %copy-done), kind=kOutput, calls=%fused_computation.9 | convolution fusion | flops 4832624640 | bytes 14155776 | tf_op jit(solution)/shard_map/pd,dhc->phc/dot_general | solution.py:23
  127.3 1.1 copy-done.1
  128.6 1.7 copy.2775
  130.3 10.3 %all-to-all-start = ((bf16[1,512,2,384]{3,2,0,1:T(2,128)(2,1)}), bf16[1,512,2,384]{3,2,0,1:T(2,128)(2,1)}, u32[]{:S(2)}, u32[]{:S(2)}) async-start(bf16[1,512,2,384]{3,2,0,1:T(2,128)(2,1)} %copy.2775), calls=%async_computation | async-start | bytes 1572864 | tf_op jit(solution)/shard_map/all_to_all | solution.py:46
  140.7 0.7 all-gather.5.cloned.1.call-update
  141.5 23.1 %all-to-all-done = bf16[1,512,2,384]{3,2,0,1:T(2,128)(2,1)} async-done(((bf16[1,512,2,384]{3,2,0,1:T(2,128)(2,1)}), bf16[1,512,2,384]{3,2,0,1:T(2,128)(2,1)}, u32[]{:S(2)}, u32[]{:S(2)}) %all-to-all-start) | async-done | bytes 786464 | tf_op jit(solution)/shard_map/all_to_all | solution.py:46
  164.5 1.2 copy.2988
  165.8 0.8 fusion.51
  167.0 0.6 copy-done.3
  167.7 1.6 fusion.11
  169.8 0.6 constant_dynamic-update-slice_fusion.63
  171.6 0.6 constant_dynamic-update-slice_fusion.60
  172.2 0.6 constant_dynamic-update-slice_fusion.59
  174.5 0.6 constant_dynamic-update-slice_fusion.55
  175.1 0.6 constant_dynamic-update-slice_fusion.54
  177.5 0.6 constant_dynamic-update-slice_fusion.50
  178.1 0.6 constant_dynamic-update-slice_fusion.49
  179.9 0.6 constant_dynamic-update-slice_fusion.46
  180.5 0.6 constant_dynamic-update-slice_fusion.45
  181.1 0.6 constant_dynamic-update-slice_fusion.44
  182.9 0.6 constant_dynamic-update-slice_fusion.41
  183.5 0.6 constant_dynamic-update-slice_fusion.40
  185.9 0.6 constant_dynamic-update-slice_fusion.36
  186.5 0.6 constant_dynamic-update-slice_fusion.35
  188.9 0.6 constant_dynamic-update-slice_fusion.31
  189.5 0.6 constant_dynamic-update-slice_fusion.30
  190.1 0.6 constant_dynamic-update-slice_fusion.29
  190.7 0.6 constant_dynamic-update-slice_fusion.28
  191.3 0.6 constant_dynamic-update-slice_fusion.27
  191.9 0.6 constant_dynamic-update-slice_fusion.26
  192.5 0.6 constant_dynamic-update-slice_fusion.25
  193.1 0.6 constant_dynamic-update-slice_fusion.24
  193.7 0.6 constant_dynamic-update-slice_fusion.23
  194.3 0.6 constant_dynamic-update-slice_fusion.22
  194.9 0.6 constant_dynamic-update-slice_fusion.21
  195.5 0.6 constant_dynamic-update-slice_fusion.20
  196.1 0.6 constant_dynamic-update-slice_fusion.19
  196.6 0.6 constant_dynamic-update-slice_fusion.18
  197.2 0.6 constant_dynamic-update-slice_fusion.17
  197.8 0.6 constant_dynamic-update-slice_fusion.16
  198.4 0.6 constant_dynamic-update-slice_fusion.15
  199.0 0.6 constant_dynamic-update-slice_fusion.14
  199.6 0.6 constant_dynamic-update-slice_fusion.13
  200.2 0.6 constant_dynamic-update-slice_fusion.12
  200.8 0.6 constant_dynamic-update-slice_fusion.11
  201.4 0.6 constant_dynamic-update-slice_fusion.10
  202.0 0.6 constant_dynamic-update-slice_fusion.9
  202.6 0.6 constant_dynamic-update-slice_fusion.8
  203.2 0.6 constant_dynamic-update-slice_fusion.7
  203.8 0.6 constant_dynamic-update-slice_fusion.6
  204.4 0.6 constant_dynamic-update-slice_fusion.5
  205.0 0.6 constant_dynamic-update-slice_fusion.4
  205.6 0.6 constant_dynamic-update-slice_fusion.3
  206.8 0.6 constant_dynamic-update-slice_fusion.1
  208.0 6.6 %all-to-all-start.1 = ((bf16[64,1,8,2,128]{4,3,2,1,0:T(2,128)(2,1)}), bf16[64,1,8,2,128]{4,3,2,1,0:T(2,128)(2,1)S(1)}, u32[]{:S(2)}, u32[]{:S(2)}) async-start(bf16[64,1,8,2,128]{4,3,2,1,0:T(2,128)(2,1)} %constant_dynamic-update-slice_fusion), calls=%async_computation.1 | async-start | bytes 524288 | tf_op jit(solution)/shard_map/all_to_all | solution.py:58
  214.7 1.8 fusion.57
  216.5 3.0 %fusion.12 = bf16[512,2,128]{0,2,1:T(8,128)(2,1)} fusion(f32[2,512]{1,0:T(2,128)S(1)} %fusion.57, bf16[512,4,384]{2,0,1:T(8,128)(2,1)} %copy-done.1), kind=kOutput, calls=%fused_computation.17 | convolution fusion | flops 270665216 | bytes 1052672 | tf_op jit(solution)/shard_map/hqk,khc->qhc/dot_general | solution.py:42
  219.5 11.6 %all-to-all-done.1 = bf16[64,1,8,2,128]{4,3,2,1,0:T(2,128)(2,1)S(1)} async-done(((bf16[64,1,8,2,128]{4,3,2,1,0:T(2,128)(2,1)}), bf16[64,1,8,2,128]{4,3,2,1,0:T(2,128)(2,1)S(1)}, u32[]{:S(2)}, u32[]{:S(2)}) %all-to-all-start.1) | async-done | bytes 262176 | tf_op jit(solution)/shard_map/all_to_all | solution.py:58
  231.1 0.9 copy.2844
  232.0 1.9 pad_maximum_fusion
  233.8 5.6 %convolution_convert_fusion = bf16[512,3072]{1,0:T(8,128)(2,1)} fusion(bf16[512,512]{0,1:T(8,128)(2,1)} %bitcast.154, bf16[3072,512]{1,0:T(8,128)(2,1)} %all-gather.5.cloned.1.call-done), kind=kOutput, calls=%fused_computation.2 | convolution fusion | flops 1612185600 | bytes 6815744 | tf_op jit(solution)/shard_map/dot_general | solution.py:71
  239.5 39.3 %reduce-scatter.2.cloned.1.call-done = bf16[64,3072]{1,0:T(8,128)(2,1)} async-done(((bf16[512,3072]{1,0:T(8,128)(2,1)}), bf16[64,3072]{1,0:T(8,128)(2,1)}) %reduce-scatter.2.cloned.1.call-update) | async-done | bytes 393232 | tf_op jit(solution)/shard_map/reduce_scatter | solution.py:70
  (56 shorter events, 13.1 us)
Async XLA Ops:
  6.5 113.0 %copy-start = (bf16[1,512,3072]{2,1,0:T(8,128)(2,1)S(1)}, bf16[1,512,3072]{2,1,0:T(8,128)(2,1)}, u32[]{:S(2)}) copy-start(bf16[1,512,3072]{2,1,0:T(8,128)(2,1)} %param.4) | copy-start | bytes 9437188
  6.5 113.0 %all-gather.3.cloned.1.call-start = ((), (), s32[]{:S(2)}) async-start(), calls=%async_computation.3 | async-start | bytes 9584640 | tf_op jit(solution)/shard_map/all_gather | solution.py:26
  127.3 1.2 copy-start.1
  128.5 12.9 %copy-start.2 = (s32[64]{0:T(128)S(1)}, s32[64]{0:T(128)}, u32[]{:S(2)}) copy-start(s32[64]{0:T(128)} %param.7) | copy-start | bytes 772
  130.3 34.2 %all-to-all-start = ((bf16[1,512,2,384]{3,2,0,1:T(2,128)(2,1)}), bf16[1,512,2,384]{3,2,0,1:T(2,128)(2,1)}, u32[]{:S(2)}, u32[]{:S(2)}) async-start(bf16[1,512,2,384]{3,2,0,1:T(2,128)(2,1)} %copy.2775), calls=%async_computation | async-start | bytes 1572864 | tf_op jit(solution)/shard_map/all_to_all | solution.py:46
  140.6 93.2 %all-gather.5.cloned.1.call-start = ((), (), s32[]{:S(2)}) async-start(), calls=%async_computation.4 | async-start | bytes 3194880 | tf_op jit(solution)/shard_map/all_gather | solution.py:29
  166.9 0.8 copy-start.3
  208.0 23.0 %all-to-all-start.1 = ((bf16[64,1,8,2,128]{4,3,2,1,0:T(2,128)(2,1)}), bf16[64,1,8,2,128]{4,3,2,1,0:T(2,128)(2,1)S(1)}, u32[]{:S(2)}, u32[]{:S(2)}) async-start(bf16[64,1,8,2,128]{4,3,2,1,0:T(2,128)(2,1)} %constant_dynamic-update-slice_fusion), calls=%async_computation.1 | async-start | bytes 524288 | tf_op jit(solution)/shard_map/all_to_all | solution.py:58
  214.6 64.1 %reduce-scatter.2.cloned.1.call-start = ((), (), s32[]{:S(2)}) async-start(), calls=%async_computation.5 | async-start | bytes 3538944 | tf_op jit(solution)/shard_map/reduce_scatter | solution.py:70
Sparse Core Ops, SparseCore 0:
  10.4 109.0 all-gather.2
  144.5 89.3 all-gather.4
  239.6 39.1 reduce-scatter.1
